TPU v7x, 32 devices: a whole 2x2x4 slice. The times are simulated.
32 devices in a mesh: cons: 4 (over y, core), prod: 8 (over z, x).
Axes of the slice: x: 2, y: 2, z: 4, core: 2. Of those that a mesh axis runs over, the one named last changes fastest.
Arguments:
- tastes: bfloat16 [16384, 128], P('cons'), may hold values from -128 to 128
- price_coef: float32 [16384], P('cons'), may hold values from 0.5 to 5
- characteristics: bfloat16 [16384, 128], P('prod'), may hold values from -6 to 6
- mean_utility: float32 [16384], P('prod'), may hold values from -4 to 4
- panel_cols: int32 [256], replicated, may hold values from 0 to 16383
- firm_map: int32 [16384], P('prod'), may hold values from 0 to 16383, as said below
- inverses: float32 [128, 128, 128], P('prod'), may hold values from -0.5 to 0.5
Outputs:
- shares: float32 [16384], P('prod')
- markup: float32 [16384], P('prod')
- response: float32 [16384, 256], P('prod')
Inputs may be any that keep to these rules, and one draw needn't show every extreme that they name: `firm_map`: a permutation of the products; the rows of firm order held by each index of prod name exactly 256 products held by each index of prod.
All inputs are finite; a program needn't handle non-finite values.
Results may differ from a plain program's by a relative error of at most 0.002.
The roundings to bfloat16 on the way count: a program that leaves them out, or rounds other values in their place, can miss the bound.
Values may be sent and summed in bfloat16 or wider, within the bound.
A program may use at most 64 MiB of HBM per device.

v0:
```python
import jax
import jax.numpy as jnp
from jax import lax
from jax.sharding import PartitionSpec as P


def utilities(taste_block, characteristics, mean_utility):
    return (
        jnp.einsum("ik,jk->ij", taste_block, characteristics, preferred_element_type=jnp.float32)
        + mean_utility[None, :]
    )


def request_order(firm_map):
    local_count = firm_map.shape[0]
    holders = lax.axis_size("prod")
    per_pair = local_count // holders
    source = firm_map // local_count
    order = jnp.argsort(source, stable=True)
    wanted = firm_map[order].reshape(holders, per_pair)
    return (order, wanted)


def regroup(jacobian, shares, firm_map):
    local_count = jacobian.shape[0]
    order, wanted = request_order(firm_map)
    base = lax.axis_index("prod") * local_count
    local_ids = lax.all_to_all(wanted, "prod", split_axis=0, concat_axis=0, tiled=True) - base
    rows_out = jnp.take(jacobian, local_ids, axis=0)
    values_out = jnp.take(shares, local_ids, axis=0)
    rows_back = lax.all_to_all(rows_out, "prod", split_axis=0, concat_axis=0, tiled=True)
    values_back = lax.all_to_all(values_out, "prod", split_axis=0, concat_axis=0, tiled=True)
    flat_rows = rows_back.reshape(local_count, jacobian.shape[1])
    flat_values = values_back.reshape(local_count)
    placed_rows = jnp.zeros_like(flat_rows).at[order].set(flat_rows)
    placed_values = jnp.zeros_like(flat_values).at[order].set(flat_values)
    return (placed_rows, placed_values)


def apply_blocks(inverses, placed_rows, placed_values):
    firm_count, block_size = (inverses.shape[0], inverses.shape[1])
    ordered = placed_rows.reshape(firm_count, block_size, placed_rows.shape[1])
    response = jnp.einsum(
        "fab,fbc->fac", inverses, ordered, precision=lax.Precision.HIGHEST
    ).reshape(placed_rows.shape)
    markup = jnp.einsum(
        "fab,fb->fa",
        inverses,
        placed_values.reshape(firm_count, block_size),
        precision=lax.Precision.HIGHEST,
    ).reshape(placed_values.shape)
    return (response, markup)


def body(tastes, price_coef, characteristics, mean_utility, panel_cols, firm_map, inverses):
    local_products = characteristics.shape[0]
    local_consumers = tastes.shape[0]
    col_count = panel_cols.shape[0]
    count_products = local_products * lax.axis_size("prod")
    count_consumers = local_consumers * lax.axis_size("cons")
    product_ids = lax.axis_index("prod") * local_products + lax.iota(jnp.int32, local_products)
    hits = product_ids[None, :] == panel_cols[:, None]
    part_chars = jnp.dot(
        hits.astype(jnp.bfloat16), characteristics, preferred_element_type=jnp.float32
    )
    part_means = jnp.dot(hits.astype(jnp.float32), mean_utility, precision=lax.Precision.HIGHEST)
    col_chars, col_means = lax.psum((part_chars, part_means), "prod")
    used_chars, used_means, used_ids = (characteristics, mean_utility, product_ids)
    block_rows = min(512, local_consumers)
    block_count = local_consumers // block_rows
    taste_blocks = tastes.reshape(block_count, block_rows, tastes.shape[1])
    coef_blocks = price_coef.reshape(block_count, block_rows)

    def local_peak(taste_block):
        utility = utilities(taste_block, used_chars, used_means)
        return jnp.maximum(jnp.max(utility, axis=1), 0.0)

    highest = lax.pmax(lax.map(local_peak, taste_blocks).reshape(local_consumers), "prod")

    def local_sum(inputs):
        taste_block, peak_block = inputs
        utility = utilities(taste_block, used_chars, used_means)
        return jnp.sum(jnp.exp(utility - peak_block[:, None]), axis=1)

    partial_total = lax.map(local_sum, (taste_blocks, highest.reshape(block_count, block_rows)))
    total = lax.psum(partial_total.reshape(local_consumers), "prod")
    denominator = jnp.exp(-highest) + total

    def consume(state_now, inputs):
        panel_sum, share_sum, diag_sum = state_now
        taste_block, coef_block, peak_block, denom_block = inputs
        utility = utilities(taste_block, used_chars, used_means)
        scaled = count_products * jnp.exp(utility - peak_block[:, None]) / denom_block[:, None]
        share_sum = share_sum + jnp.sum(scaled, axis=0)
        diag_sum = diag_sum + jnp.dot(coef_block, scaled, precision=lax.Precision.HIGHEST)
        col_util = (
            jnp.dot(taste_block.astype(jnp.float32), col_chars.T, precision=lax.Precision.HIGHEST)
            + col_means[None, :]
        )
        col_scaled = count_products * jnp.exp(col_util - peak_block[:, None]) / denom_block[:, None]
        weighted = (coef_block[:, None] * col_scaled).astype(jnp.bfloat16)
        panel_sum = panel_sum + lax.dot_general(
            scaled.astype(jnp.bfloat16),
            weighted,
            (((0,), (0,)), ((), ())),
            preferred_element_type=jnp.float32,
        )
        return ((panel_sum, share_sum, diag_sum), None)

    start_state = (
        jnp.zeros((local_products, col_count), jnp.float32),
        jnp.zeros((local_products,), jnp.float32),
        jnp.zeros((local_products,), jnp.float32),
    )
    scan_inputs = (
        taste_blocks,
        coef_blocks,
        highest.reshape(block_count, block_rows),
        denominator.reshape(block_count, block_rows),
    )
    (panel_sum, share_sum, diag_sum), _ = lax.scan(consume, start_state, scan_inputs)
    marks = (used_ids[:, None] == panel_cols[None, :]).astype(jnp.float32)
    part_cols = col_count // lax.axis_size("cons")
    panel_part = lax.psum_scatter(panel_sum, "cons", scatter_dimension=1, tiled=True)
    share_all, diag_all = lax.psum((share_sum, diag_sum), "cons")
    mark_part = lax.dynamic_slice_in_dim(marks, lax.axis_index("cons") * part_cols, part_cols, 1)
    local_shares = share_all / count_consumers
    diagonal = diag_all / count_consumers
    jacobian = panel_part / count_consumers - diagonal[:, None] * mark_part
    placed_rows, placed_values = regroup(jacobian, local_shares, firm_map)
    response, markup = apply_blocks(inverses, placed_rows, placed_values)
    response = lax.all_gather(response, "cons", axis=1, tiled=True)
    return (local_shares, markup, response)


def solution(mesh):
    return jax.shard_map(
        body,
        mesh=mesh,
        in_specs=(
            P("cons", None),
            P("cons"),
            P("prod", None),
            P("prod"),
            P(),
            P("prod"),
            P("prod", None, None),
        ),
        out_specs=(P("prod"), P("prod"), P("prod", None)),
        check_vma=False,
    )
```

profile of v0, /device:TPU:0, one launch (start us, length us, event | category | flops | bytes accessed | tf_op | source)
XLA Modules:
  0.0 332.7 jit_solution(9404396025365228283)
XLA Ops:
  7.2 2.3 fusion.23
  9.6 15.6 %while.35 = (s32[]{:T(128)}, f32[8,512]{1,0:T(8,128)S(1)}, bf16[8,512,128]{2,1,0:T(8,128)(2,1)}, bf16[2048,128]{1,0:T(8,128)(2,1)}, f32[2048]{0:T(1024)}, /*index=5*/s32[]{:T(128)}, s32[]{:T(128)}) while((s32[]{:T(128)}, f32[8,512]{1,0:T(8,128)S(1)}, bf16[8,512,128]{2,1,0:T(8,128)(2,1)}, bf16[2048,128]{1,0:T(8,128)(2,1)}, f32[2048]{0:T(1024)}, ...), condition=%wide.region_2.3_spmd, body=%wide.region_0.2_spmd.sunk | while | flops 270532608 | bytes 674385 | solution.py:78
  13.5 1.9 add_reduce_fusion.2
  17.4 1.9 add_reduce_fusion.2
  19.4 1.9 add_reduce_fusion.2
  21.3 1.9 add_reduce_fusion.2
  25.3 38.9 %pmax.7 = f32[4096]{0:T(1024)S(1)} all-reduce(f32[4096]{0:T(1024)S(1)} %bitcast.120), channel_id=1, replica_groups=mesh['cons'=4,'prod'=8] {'prod'}, use_global_device_ids=true, to_apply=%region_3.0 | all-reduce | flops 4096 | bytes 32768 | tf_op jit(solution)/shard_map/pmax | solution.py:78
  64.1 16.9 %while.36 = (s32[]{:T(128)}, f32[8,512]{1,0:T(8,128)S(1)}, bf16[8,512,128]{2,1,0:T(8,128)(2,1)}, bf16[2048,128]{1,0:T(8,128)(2,1)}, f32[2048]{0:T(1024)}, /*index=5*/f32[8,512]{1,0:T(8,128)S(1)}, s32[]{:T(128)}, s32[]{:T(128)}) while((s32[]{:T(128)}, f32[8,512]{1,0:T(8,128)S(1)}, bf16[8,512,128]{2,1,0:T(8,128)(2,1)}, ...), condition=%wide.region_6.7_spmd, body=%wide.region_4.6_spmd.sunk | while | flops 271580672 | bytes 676445 | solution.py:85
  64.2 2.0 exponential_reduce_fusion.2
  66.3 2.0 exponential_reduce_fusion.2
  68.4 2.0 exponential_reduce_fusion.2
  70.5 2.0 exponential_reduce_fusion.2
  72.6 2.0 exponential_reduce_fusion.2
  74.7 2.0 exponential_reduce_fusion.2
  76.8 2.0 exponential_reduce_fusion.2
  79.0 2.0 exponential_reduce_fusion.2
  82.8 33.0 %all-reduce = (f32[4096]{0:T(1024)S(1)}, f32[256]{0:T(256)S(1)}) all-reduce(f32[4096]{0:T(1024)S(1)} %bitcast.119, f32[256]{0:T(256)S(1)} %bitcast.132), channel_id=1, replica_groups=mesh['cons'=4,'prod'=8] {'prod'}, use_global_device_ids=true, to_apply=%region_7.8 | all-reduce | flops 4352 | bytes 34816 | tf_op jit(solution)/shard_map/psum | solution.py:86
  115.9 93.8 %while.37 = (s32[]{:T(128)}, f32[2048,256]{1,0:T(8,128)S(1)}, f32[2048]{0:T(1024)S(1)}, f32[2048]{0:T(1024)S(1)}, bf16[8,512,128]{2,1,0:T(8,128)(2,1)}, /*index=...) while((s32[]{:T(128)}, f32[2048,256]{1,0:T(8,128)S(1)}, ...), condition=%wide.region_12.13_spmd.clone, body=%wide.region_10.12_spmd.clone.sunk | while | flops 1027348480 | bytes 35621072 | solution.py:121
  115.9 2.3 fusion.75
  118.3 1.9 copy-done.3
  120.1 2.1 fusion.76
  123.6 4.0 %convolution_add_fusion.3 = f32[2048,256]{1,0:T(8,128)S(1)} fusion(bf16[512,256]{1,0:T(8,128)(2,1)S(1)} %fusion.74, f32[2048,256]{1,0:T(8,128)S(1)} %get-tuple-element.451, f32[512,2048]{1,0:T(8,128)} %copy-done.3, pred[]{:T(512)S(6)} %compare.9), kind=kOutput, calls=%fused_computation.16.clone.1 | convolution fusion | flops 538968064 | bytes 8650753 | tf_op jit(solution)/shard_map/while/body/eval_jaxpr/dot_general | solution.py:102
  127.6 2.3 fusion.75
  130.0 1.9 copy-done.3
  131.9 2.1 fusion.76
  135.3 4.0 %convolution_add_fusion.3 = f32[2048,256]{1,0:T(8,128)S(1)} fusion(bf16[512,256]{1,0:T(8,128)(2,1)S(1)} %fusion.74, f32[2048,256]{1,0:T(8,128)S(1)} %get-tuple-element.451, f32[512,2048]{1,0:T(8,128)} %copy-done.3, pred[]{:T(512)S(6)} %compare.9), kind=kOutput, calls=%fused_computation.16.clone.1 | convolution fusion | flops 538968064 | bytes 8650753 | tf_op jit(solution)/shard_map/while/body/eval_jaxpr/dot_general | solution.py:102
  139.4 2.3 fusion.75
  141.7 1.9 copy-done.3
  143.6 2.1 fusion.76
  147.0 4.0 %convolution_add_fusion.3 = f32[2048,256]{1,0:T(8,128)S(1)} fusion(bf16[512,256]{1,0:T(8,128)(2,1)S(1)} %fusion.74, f32[2048,256]{1,0:T(8,128)S(1)} %get-tuple-element.451, f32[512,2048]{1,0:T(8,128)} %copy-done.3, pred[]{:T(512)S(6)} %compare.9), kind=kOutput, calls=%fused_computation.16.clone.1 | convolution fusion | flops 538968064 | bytes 8650753 | tf_op jit(solution)/shard_map/while/body/eval_jaxpr/dot_general | solution.py:102
  151.1 2.3 fusion.75
  153.4 1.9 copy-done.3
  155.3 2.1 fusion.76
  158.8 4.0 %convolution_add_fusion.3 = f32[2048,256]{1,0:T(8,128)S(1)} fusion(bf16[512,256]{1,0:T(8,128)(2,1)S(1)} %fusion.74, f32[2048,256]{1,0:T(8,128)S(1)} %get-tuple-element.451, f32[512,2048]{1,0:T(8,128)} %copy-done.3, pred[]{:T(512)S(6)} %compare.9), kind=kOutput, calls=%fused_computation.16.clone.1 | convolution fusion | flops 538968064 | bytes 8650753 | tf_op jit(solution)/shard_map/while/body/eval_jaxpr/dot_general | solution.py:102
  162.8 2.3 fusion.75
  165.1 1.9 copy-done.3
  167.0 2.1 fusion.76
  170.5 4.0 %convolution_add_fusion.3 = f32[2048,256]{1,0:T(8,128)S(1)} fusion(bf16[512,256]{1,0:T(8,128)(2,1)S(1)} %fusion.74, f32[2048,256]{1,0:T(8,128)S(1)} %get-tuple-element.451, f32[512,2048]{1,0:T(8,128)} %copy-done.3, pred[]{:T(512)S(6)} %compare.9), kind=kOutput, calls=%fused_computation.16.clone.1 | convolution fusion | flops 538968064 | bytes 8650753 | tf_op jit(solution)/shard_map/while/body/eval_jaxpr/dot_general | solution.py:102
  174.5 2.3 fusion.75
  176.9 1.9 copy-done.3
  178.7 2.1 fusion.76
  182.2 4.0 %convolution_add_fusion.3 = f32[2048,256]{1,0:T(8,128)S(1)} fusion(bf16[512,256]{1,0:T(8,128)(2,1)S(1)} %fusion.74, f32[2048,256]{1,0:T(8,128)S(1)} %get-tuple-element.451, f32[512,2048]{1,0:T(8,128)} %copy-done.3, pred[]{:T(512)S(6)} %compare.9), kind=kOutput, calls=%fused_computation.16.clone.1 | convolution fusion | flops 538968064 | bytes 8650753 | tf_op jit(solution)/shard_map/while/body/eval_jaxpr/dot_general | solution.py:102
  186.3 2.3 fusion.75
  188.6 1.9 copy-done.3
  190.5 2.1 fusion.76
  193.9 4.0 %convolution_add_fusion.3 = f32[2048,256]{1,0:T(8,128)S(1)} fusion(bf16[512,256]{1,0:T(8,128)(2,1)S(1)} %fusion.74, f32[2048,256]{1,0:T(8,128)S(1)} %get-tuple-element.451, f32[512,2048]{1,0:T(8,128)} %copy-done.3, pred[]{:T(512)S(6)} %compare.9), kind=kOutput, calls=%fused_computation.16.clone.1 | convolution fusion | flops 538968064 | bytes 8650753 | tf_op jit(solution)/shard_map/while/body/eval_jaxpr/dot_general | solution.py:102
  198.0 2.3 fusion.75
  200.3 1.9 copy-done.3
  202.2 2.1 fusion.76
  205.6 4.0 %convolution_add_fusion.3 = f32[2048,256]{1,0:T(8,128)S(1)} fusion(bf16[512,256]{1,0:T(8,128)(2,1)S(1)} %fusion.74, f32[2048,256]{1,0:T(8,128)S(1)} %get-tuple-element.451, f32[512,2048]{1,0:T(8,128)} %copy-done.3, pred[]{:T(512)S(6)} %compare.9), kind=kOutput, calls=%fused_computation.16.clone.1 | convolution fusion | flops 538968064 | bytes 8650753 | tf_op jit(solution)/shard_map/while/body/eval_jaxpr/dot_general | solution.py:102
  211.5 5.0 %sort.17 = (s32[2048]{0:T(1024)}, s32[2048]{0:T(1024)S(1)}) sort(s32[2048]{0:T(1024)S(1)} %add_select_fusion, s32[2048]{0:T(1024)S(1)} %iota.12), dimensions={0}, to_apply=%region_14.15 | sort | flops 22528 | bytes 32768 | tf_op jit(solution)/shard_map/jit(argsort)/sort | solution.py:19
  216.6 20.5 %gather_fusion = s32[2048]{0:T(1024)} fusion(s32[2048]{0:T(1024)S(1)} %copy-done.1, s32[2048]{0:T(1024)S(1)} %get-tuple-element.240), kind=kCustom, calls=%fused_computation | custom fusion | bytes 24576 | tf_op jit(solution)/shard_map/gather | solution.py:20
  237.1 3.3 %all-to-all-start = ((s32[8,1,256]{2,1,0:T(1,128)}), s32[8,1,256]{2,1,0:T(1,128)S(1)}, u32[]{:S(2)}, u32[]{:S(2)}) async-start(s32[8,1,256]{2,1,0:T(1,128)} %bitcast.8), calls=%async_computation | async-start | bytes 16384 | tf_op jit(solution)/shard_map/all_to_all | solution.py:28
  240.6 6.3 %all-to-all-done = s32[8,1,256]{2,1,0:T(1,128)S(1)} async-done(((s32[8,1,256]{2,1,0:T(1,128)}), s32[8,1,256]{2,1,0:T(1,128)S(1)}, u32[]{:S(2)}, u32[]{:S(2)}) %all-to-all-start) | async-done | bytes 8224 | tf_op jit(solution)/shard_map/all_to_all | solution.py:28
  247.0 10.3 %all-reduce.1 = (f32[2048]{0:T(1024)S(1)}, f32[2048]{0:T(1024)S(1)}) all-reduce(f32[2048]{0:T(1024)S(1)} %get-tuple-element.129, f32[2048]{0:T(1024)S(1)} %get-tuple-element.132), channel_id=1, replica_groups=mesh['cons'=4,'prod'=8] {'cons'}, use_global_device_ids=true, to_apply=%region_13.14 | all-reduce | flops 4096 | bytes 32768 | tf_op jit(solution)/shard_map/psum | solution.py:125
  259.4 5.5 %gather_fusion.2 = f32[2048,64]{1,0:T(8,128)S(1)} fusion(f32[2048,64]{1,0:T(8,128)S(1)} %multiply_subtract_fusion, s32[2048]{0:T(1024)S(1)} %broadcast_clamp_fusion), kind=kCustom, calls=%fused_computation.2 | custom fusion | bytes 1056768 | tf_op jit(solution)/shard_map/jit(_take)/gather | solution.py:29
  265.3 16.7 %all_to_all.20 = f32[8,256,64]{1,2,0:T(8,128)S(1)} all-to-all(f32[8,256,64]{1,2,0:T(8,128)S(1)} %broadcast_select_fusion), channel_id=1, replica_groups=mesh['cons'=4,'prod'=8] {'prod'}, dimensions={0} | all-to-all | bytes 1048576 | tf_op jit(solution)/shard_map/all_to_all | solution.py:31
  282.3 5.8 %scatter_custom_fusion.1 = f32[2048,64]{1,0:T(8,128)S(1)} fusion(s32[2048]{0:T(1024)S(1)} %get-tuple-element.241, f32[2048,64]{1,0:T(8,128)S(1)} %bitcast.112, f32[]{:T(128)} %constant.94.clone.1), kind=kCustom, calls=%fused_computation.49 | custom fusion | bytes 524292 | tf_op jit(solution)/shard_map/scatter | solution.py:35
  288.1 2.0 convolution_bitcast_fusion
  291.1 11.8 %gather_fusion.1 = f32[2048]{0:T(1024)S(1)} fusion(f32[2048]{0:T(1024)S(1)} %broadcast_multiply_fusion.1, s32[2048]{0:T(1024)S(1)} %broadcast_clamp_fusion), kind=kCustom, calls=%fused_computation.1 | custom fusion | bytes 24576 | tf_op jit(solution)/shard_map/jit(_take)/gather | solution.py:30
  302.9 9.9 %all_to_all.21 = f32[8,1,256]{2,1,0:T(1,128)S(1)} all-to-all(f32[8,1,256]{2,1,0:T(1,128)S(1)} %and_select_fusion), channel_id=1, replica_groups=mesh['cons'=4,'prod'=8] {'prod'}, dimensions={0} | all-to-all | bytes 16384 | tf_op jit(solution)/shard_map/all_to_all | solution.py:32
  312.8 8.0 %scatter_custom_fusion = f32[2048]{0:T(1024)S(1)} fusion(s32[2048]{0:T(1024)S(1)} %get-tuple-element.241, f32[2048]{0:T(1024)S(1)} %bitcast.131, f32[]{:T(128)} %constant.94.clone.1), kind=kCustom, calls=%fused_computation.72 | custom fusion | bytes 8196 | tf_op jit(solution)/shard_map/scatter | solution.py:36
  320.9 2.3 fusion.36
  323.3 2.9 copy.29
  (149 shorter events, 27.3 us)
Async XLA Ops:
  7.2 281.0 %copy-start = (f32[16,128,128]{2,1,0:T(8,128)S(1)}, f32[16,128,128]{2,1,0:T(8,128)}, u32[]{:S(2)}) copy-start(f32[16,128,128]{2,1,0:T(8,128)} %param.19) | copy-start | bytes 3145732
  7.2 108.7 %all-reduce.4.cloned.1.call-start = ((), (), s32[]{:S(2)}) async-start(), calls=%async_computation.4 | async-start | bytes 262144 | tf_op jit(solution)/shard_map/psum | solution.py:67
  9.5 247.8 %reduce-scatter.4.cloned.1.call-start = ((), (), s32[]{:S(2)}) async-start(), calls=%async_computation.6 | async-start | bytes 2621440
  64.1 16.9 %copy-start.6 = (s32[256]{0:T(256)S(1)}, s32[256]{0:T(256)}, u32[]{:S(2)}) copy-start(s32[256]{0:T(256)} %param.17) | copy-start | bytes 3076
  64.1 51.7 %copy-start.4 = (f32[4096]{0:T(1024)S(1)}, f32[4096]{0:T(1024)}, u32[]{:S(2)}) copy-start(f32[4096]{0:T(1024)} %param.14) | copy-start | bytes 49156
  118.2 1.9 copy-start.3
  118.2 4.0 %copy-start.5 = (f32[256,128]{1,0:T(8,128)S(1)}, f32[256,128]{1,0:T(8,128)}, u32[]{:S(2)}) copy-start(f32[256,128]{1,0:T(8,128)} %get-tuple-element.474) | copy-start | bytes 393220 | tf_op jit(solution)/shard_map/while
  129.9 1.9 copy-start.3
  129.9 4.0 %copy-start.5 = (f32[256,128]{1,0:T(8,128)S(1)}, f32[256,128]{1,0:T(8,128)}, u32[]{:S(2)}) copy-start(f32[256,128]{1,0:T(8,128)} %get-tuple-element.474) | copy-start | bytes 393220 | tf_op jit(solution)/shard_map/while
  141.7 1.9 copy-start.3
  141.7 4.0 %copy-start.5 = (f32[256,128]{1,0:T(8,128)S(1)}, f32[256,128]{1,0:T(8,128)}, u32[]{:S(2)}) copy-start(f32[256,128]{1,0:T(8,128)} %get-tuple-element.474) | copy-start | bytes 393220 | tf_op jit(solution)/shard_map/while
  153.4 1.9 copy-start.3
  153.4 4.0 %copy-start.5 = (f32[256,128]{1,0:T(8,128)S(1)}, f32[256,128]{1,0:T(8,128)}, u32[]{:S(2)}) copy-start(f32[256,128]{1,0:T(8,128)} %get-tuple-element.474) | copy-start | bytes 393220 | tf_op jit(solution)/shard_map/while
  165.1 1.9 copy-start.3
  165.1 4.0 %copy-start.5 = (f32[256,128]{1,0:T(8,128)S(1)}, f32[256,128]{1,0:T(8,128)}, u32[]{:S(2)}) copy-start(f32[256,128]{1,0:T(8,128)} %get-tuple-element.474) | copy-start | bytes 393220 | tf_op jit(solution)/shard_map/while
  176.8 1.9 copy-start.3
  176.8 4.0 %copy-start.5 = (f32[256,128]{1,0:T(8,128)S(1)}, f32[256,128]{1,0:T(8,128)}, u32[]{:S(2)}) copy-start(f32[256,128]{1,0:T(8,128)} %get-tuple-element.474) | copy-start | bytes 393220 | tf_op jit(solution)/shard_map/while
  188.5 1.9 copy-start.3
  188.6 4.0 %copy-start.5 = (f32[256,128]{1,0:T(8,128)S(1)}, f32[256,128]{1,0:T(8,128)}, u32[]{:S(2)}) copy-start(f32[256,128]{1,0:T(8,128)} %get-tuple-element.474) | copy-start | bytes 393220 | tf_op jit(solution)/shard_map/while
  200.3 1.9 copy-start.3
  200.3 4.0 %copy-start.5 = (f32[256,128]{1,0:T(8,128)S(1)}, f32[256,128]{1,0:T(8,128)}, u32[]{:S(2)}) copy-start(f32[256,128]{1,0:T(8,128)} %get-tuple-element.474) | copy-start | bytes 393220 | tf_op jit(solution)/shard_map/while
  209.7 1.9 copy-start.1
  237.1 9.8 %all-to-all-start = ((s32[8,1,256]{2,1,0:T(1,128)}), s32[8,1,256]{2,1,0:T(1,128)S(1)}, u32[]{:S(2)}, u32[]{:S(2)}) async-start(s32[8,1,256]{2,1,0:T(1,128)} %bitcast.8), calls=%async_computation | async-start | bytes 16384 | tf_op jit(solution)/shard_map/all_to_all | solution.py:28
  240.5 82.8 %all-gather.2.cloned.1.call-start = ((), (), s32[]{:S(2)}) async-start(), calls=%async_computation.5 | async-start | bytes 2621440 | tf_op jit(solution)/shard_map/all_gather | solution.py:132
  291.1 11.8 %copy-start.2 = (f32[2048]{0:T(1024)}, f32[2048]{0:T(1024)S(1)}, u32[]{:S(2)}) copy-start(f32[2048]{0:T(1024)S(1)} %broadcast_multiply_fusion.1) | copy-start | bytes 24580
Sparse Core Ops, SparseCore 0:
  11.9 73.2 all-reduce.3
  211.6 28.5 reduce-scatter.3
  291.2 20.6 all-gather.1
where the time goes:
time: 334 us; the launch traced here: 333 us
  matrix products  117 us (35%)
  blocking collectives  109 us (33%)
  local copies, waits for them, and re-layouts  75.8 us (23%)
  between operations  14.1 us (4%)
  waiting for transfers between devices  6.41 us (2%)
  other arithmetic  6 us (2%)
  starting transfers between devices  3.46 us (1%)
    dot_general x24, matrix products, utilities(): jnp.einsum('ik,jk->ij', taste_block, characteristics, preferred_element_t...  49.2 us
    pmax x1, blocking collectives, body(): lax.pmax(lax.map(local_peak, taste_blocks).reshape(local_consumers), 'prod')  38.9 us
    psum x1, blocking collectives, body(): total = lax.psum(partial_total.reshape(local_consumers), 'prod')  33 us
    dot_general x8, matrix products, consume(): lax.dot_general(scaled.astype(jnp.bfloat16), weighted, (((0,), (0,)), (()...  32 us
    gather x1, local copies, waits for them, and re-layouts, request_order(): wanted = firm_map[order].reshape(holders, per_pair)  20.5 us
    all_to_all x1, blocking collectives, regroup(): lax.all_to_all(rows_out, 'prod', split_axis=0, concat_axis=0, tiled=True)  16.7 us
    dot_general x8, matrix products, consume(): jnp.dot(coef_block, scaled, precision=lax.Precision.HIGHEST)  16.6 us
    while x32, local copies, waits for them, and re-layouts  15.2 us
  transfers between devices with their start and end apart: 4, of which 1 were waited for; matrix products, arithmetic and copies ran while one was open for 25% of the time, Pallas kernels for 0%

commit v1 on v0

--- a/solution.py
+++ b/solution.py
@@ -83,7 +83,7 @@
         return jnp.sum(jnp.exp(utility - peak_block[:, None]), axis=1)
 
     partial_total = lax.map(local_sum, (taste_blocks, highest.reshape(block_count, block_rows)))
-    total = lax.psum(partial_total.reshape(local_consumers), "prod")
+    total = jnp.sum(lax.all_gather(partial_total.reshape(local_consumers), "prod"), axis=0)
     denominator = jnp.exp(-highest) + total
 
     def consume(state_now, inputs):

time: 334 us -> 349 us (1.045)
  blocking collectives: 109 us -> 123 us
    all_gather x0 -> x1, blocking collectives: none -> 30.5 us  [body(): lax.all_gather(partial_total.reshape(local_consumers), 'prod')]
    psum x1, blocking collectives: 33 us -> 17.2 us  [body(): col_chars, col_means = lax.psum((part_chars, part_means), 'prod')]
  transfers between devices with their start and end apart: 4 -> 4, of which waited for: 1 -> 1; matrix products, arithmetic and copies ran while one was open for 25% -> 24% of each run, Pallas kernels for 0% -> 0%
where the time goes in v1:
time: 349 us; the launch traced here: 347 us
  blocking collectives  123 us (35%)
  matrix products  117 us (34%)
  local copies, waits for them, and re-layouts  75.8 us (22%)
  between operations  14.1 us (4%)
  waiting for transfers between devices  6.39 us (2%)
  other arithmetic  6.1 us (2%)
    dot_general x24, matrix products, utilities(): jnp.einsum('ik,jk->ij', taste_block, characteristics, preferred_element_t...  49.3 us
    pmax x1, blocking collectives, body(): lax.pmax(lax.map(local_peak, taste_blocks).reshape(local_consumers), 'prod')  38.9 us
    dot_general x8, matrix products, consume(): lax.dot_general(scaled.astype(jnp.bfloat16), weighted, (((0,), (0,)), (()...  32 us
    all_gather x1, blocking collectives, body(): lax.all_gather(partial_total.reshape(local_consumers), 'prod')  30.5 us
    gather x1, local copies, waits for them, and re-layouts, request_order(): wanted = firm_map[order].reshape(holders, per_pair)  20.5 us
    psum x1, blocking collectives, body(): col_chars, col_means = lax.psum((part_chars, part_means), 'prod')  17.2 us
    all_to_all x1, blocking collectives, regroup(): lax.all_to_all(rows_out, 'prod', split_axis=0, concat_axis=0, tiled=True)  16.6 us
    dot_general x8, matrix products, consume(): jnp.dot(coef_block, scaled, precision=lax.Precision.HIGHEST)  16.6 us
  transfers between devices with their start and end apart: 4, of which 1 were waited for; matrix products, arithmetic and copies ran while one was open for 24% of the time, Pallas kernels for 0%

profile of v1, /device:TPU:0, one launch (start us, length us, event | category | flops | bytes accessed | tf_op | source)
XLA Modules:
  0.0 347.5 jit_solution(17272819656009755798)
XLA Ops:
  7.2 2.3 fusion.23
  9.6 15.6 %while.35 = (s32[]{:T(128)}, f32[8,512]{1,0:T(8,128)S(1)}, bf16[8,512,128]{2,1,0:T(8,128)(2,1)}, bf16[2048,128]{1,0:T(8,128)(2,1)}, f32[2048]{0:T(1024)}, /*index=5*/s32[]{:T(128)}, s32[]{:T(128)}) while((s32[]{:T(128)}, f32[8,512]{1,0:T(8,128)S(1)}, bf16[8,512,128]{2,1,0:T(8,128)(2,1)}, bf16[2048,128]{1,0:T(8,128)(2,1)}, f32[2048]{0:T(1024)}, ...), condition=%wide.region_2.3_spmd, body=%wide.region_0.2_spmd.sunk | while | flops 270532608 | bytes 674385 | solution.py:78
  9.6 1.9 add_reduce_fusion.2
  19.4 1.9 add_reduce_fusion.2
  21.3 1.9 add_reduce_fusion.2
  25.3 38.9 %pmax.7 = f32[4096]{0:T(1024)S(1)} all-reduce(f32[4096]{0:T(1024)S(1)} %bitcast.116), channel_id=1, replica_groups=mesh['cons'=4,'prod'=8] {'prod'}, use_global_device_ids=true, to_apply=%region_3.0 | all-reduce | flops 4096 | bytes 32768 | tf_op jit(solution)/shard_map/pmax | solution.py:78
  64.1 16.9 %while.36 = (s32[]{:T(128)}, f32[8,512]{1,0:T(8,128)S(1)}, bf16[8,512,128]{2,1,0:T(8,128)(2,1)}, bf16[2048,128]{1,0:T(8,128)(2,1)}, f32[2048]{0:T(1024)}, /*index=5*/f32[8,512]{1,0:T(8,128)S(1)}, s32[]{:T(128)}, s32[]{:T(128)}) while((s32[]{:T(128)}, f32[8,512]{1,0:T(8,128)S(1)}, bf16[8,512,128]{2,1,0:T(8,128)(2,1)}, ...), condition=%wide.region_6.7_spmd, body=%wide.region_4.6_spmd.sunk | while | flops 271580672 | bytes 676445 | solution.py:85
  64.2 2.0 exponential_reduce_fusion.2
  66.3 2.0 exponential_reduce_fusion.2
  68.4 2.0 exponential_reduce_fusion.2
  70.5 2.0 exponential_reduce_fusion.2
  72.6 2.0 exponential_reduce_fusion.2
  74.7 2.0 exponential_reduce_fusion.2
  76.8 2.0 exponential_reduce_fusion.2
  79.0 2.0 exponential_reduce_fusion.2
  81.1 30.5 %all-gather = f32[8,1,4096]{2,1,0:T(1,128)S(1)} all-gather(f32[1,1,4096]{2,1,0:T(1,128)S(1)} %reshape.166), channel_id=1, replica_groups=mesh['cons'=4,'prod'=8] {'prod'}, dimensions={0}, use_global_device_ids=true | all-gather | bytes 147456 | tf_op jit(solution)/shard_map/all_gather | solution.py:86
  113.5 17.2 %psum.29 = f32[256]{0:T(256)S(1)} all-reduce(f32[256]{0:T(256)S(1)} %bitcast.128), channel_id=1, replica_groups=mesh['cons'=4,'prod'=8] {'prod'}, use_global_device_ids=true, to_apply=%region_9.10 | all-reduce | flops 256 | bytes 2048 | tf_op jit(solution)/shard_map/psum | solution.py:67
  130.7 93.8 %while.37 = (s32[]{:T(128)}, f32[2048,256]{1,0:T(8,128)S(1)}, f32[2048]{0:T(1024)S(1)}, f32[2048]{0:T(1024)S(1)}, bf16[8,512,128]{2,1,0:T(8,128)(2,1)}, /*index=...) while((s32[]{:T(128)}, f32[2048,256]{1,0:T(8,128)S(1)}, ...), condition=%wide.region_12.13_spmd.clone, body=%wide.region_10.12_spmd.clone.sunk | while | flops 1027348480 | bytes 35621072 | solution.py:121
  130.7 2.3 fusion.75
  133.1 1.9 copy-done.3
  134.9 2.1 fusion.76
  138.4 4.0 %convolution_add_fusion.3 = f32[2048,256]{1,0:T(8,128)S(1)} fusion(bf16[512,256]{1,0:T(8,128)(2,1)S(1)} %fusion.74, f32[2048,256]{1,0:T(8,128)S(1)} %get-tuple-element.449, f32[512,2048]{1,0:T(8,128)} %copy-done.3, pred[]{:T(512)S(6)} %compare.9), kind=kOutput, calls=%fused_computation.16.clone.1 | convolution fusion | flops 538968064 | bytes 8650753 | tf_op jit(solution)/shard_map/while/body/eval_jaxpr/dot_general | solution.py:102
  142.4 2.3 fusion.75
  144.8 1.9 copy-done.3
  146.7 2.1 fusion.76
  150.1 4.0 %convolution_add_fusion.3 = f32[2048,256]{1,0:T(8,128)S(1)} fusion(bf16[512,256]{1,0:T(8,128)(2,1)S(1)} %fusion.74, f32[2048,256]{1,0:T(8,128)S(1)} %get-tuple-element.449, f32[512,2048]{1,0:T(8,128)} %copy-done.3, pred[]{:T(512)S(6)} %compare.9), kind=kOutput, calls=%fused_computation.16.clone.1 | convolution fusion | flops 538968064 | bytes 8650753 | tf_op jit(solution)/shard_map/while/body/eval_jaxpr/dot_general | solution.py:102
  154.2 2.3 fusion.75
  156.5 1.9 copy-done.3
  158.4 2.1 fusion.76
  161.9 4.0 %convolution_add_fusion.3 = f32[2048,256]{1,0:T(8,128)S(1)} fusion(bf16[512,256]{1,0:T(8,128)(2,1)S(1)} %fusion.74, f32[2048,256]{1,0:T(8,128)S(1)} %get-tuple-element.449, f32[512,2048]{1,0:T(8,128)} %copy-done.3, pred[]{:T(512)S(6)} %compare.9), kind=kOutput, calls=%fused_computation.16.clone.1 | convolution fusion | flops 538968064 | bytes 8650753 | tf_op jit(solution)/shard_map/while/body/eval_jaxpr/dot_general | solution.py:102
  165.9 2.3 fusion.75
  168.2 1.9 copy-done.3
  170.1 2.1 fusion.76
  173.6 4.0 %convolution_add_fusion.3 = f32[2048,256]{1,0:T(8,128)S(1)} fusion(bf16[512,256]{1,0:T(8,128)(2,1)S(1)} %fusion.74, f32[2048,256]{1,0:T(8,128)S(1)} %get-tuple-element.449, f32[512,2048]{1,0:T(8,128)} %copy-done.3, pred[]{:T(512)S(6)} %compare.9), kind=kOutput, calls=%fused_computation.16.clone.1 | convolution fusion | flops 538968064 | bytes 8650753 | tf_op jit(solution)/shard_map/while/body/eval_jaxpr/dot_general | solution.py:102
  177.6 2.3 fusion.75
  180.0 1.9 copy-done.3
  181.9 2.1 fusion.76
  185.3 4.0 %convolution_add_fusion.3 = f32[2048,256]{1,0:T(8,128)S(1)} fusion(bf16[512,256]{1,0:T(8,128)(2,1)S(1)} %fusion.74, f32[2048,256]{1,0:T(8,128)S(1)} %get-tuple-element.449, f32[512,2048]{1,0:T(8,128)} %copy-done.3, pred[]{:T(512)S(6)} %compare.9), kind=kOutput, calls=%fused_computation.16.clone.1 | convolution fusion | flops 538968064 | bytes 8650753 | tf_op jit(solution)/shard_map/while/body/eval_jaxpr/dot_general | solution.py:102
  189.4 2.3 fusion.75
  191.7 1.9 copy-done.3
  193.6 2.1 fusion.76
  197.1 4.0 %convolution_add_fusion.3 = f32[2048,256]{1,0:T(8,128)S(1)} fusion(bf16[512,256]{1,0:T(8,128)(2,1)S(1)} %fusion.74, f32[2048,256]{1,0:T(8,128)S(1)} %get-tuple-element.449, f32[512,2048]{1,0:T(8,128)} %copy-done.3, pred[]{:T(512)S(6)} %compare.9), kind=kOutput, calls=%fused_computation.16.clone.1 | convolution fusion | flops 538968064 | bytes 8650753 | tf_op jit(solution)/shard_map/while/body/eval_jaxpr/dot_general | solution.py:102
  201.1 2.3 fusion.75
  203.4 1.9 copy-done.3
  205.3 2.1 fusion.76
  208.8 4.0 %convolution_add_fusion.3 = f32[2048,256]{1,0:T(8,128)S(1)} fusion(bf16[512,256]{1,0:T(8,128)(2,1)S(1)} %fusion.74, f32[2048,256]{1,0:T(8,128)S(1)} %get-tuple-element.449, f32[512,2048]{1,0:T(8,128)} %copy-done.3, pred[]{:T(512)S(6)} %compare.9), kind=kOutput, calls=%fused_computation.16.clone.1 | convolution fusion | flops 538968064 | bytes 8650753 | tf_op jit(solution)/shard_map/while/body/eval_jaxpr/dot_general | solution.py:102
  212.8 2.3 fusion.75
  215.2 1.9 copy-done.3
  217.1 2.1 fusion.76
  220.5 4.0 %convolution_add_fusion.3 = f32[2048,256]{1,0:T(8,128)S(1)} fusion(bf16[512,256]{1,0:T(8,128)(2,1)S(1)} %fusion.74, f32[2048,256]{1,0:T(8,128)S(1)} %get-tuple-element.449, f32[512,2048]{1,0:T(8,128)} %copy-done.3, pred[]{:T(512)S(6)} %compare.9), kind=kOutput, calls=%fused_computation.16.clone.1 | convolution fusion | flops 538968064 | bytes 8650753 | tf_op jit(solution)/shard_map/while/body/eval_jaxpr/dot_general | solution.py:102
  226.4 5.0 %sort.17 = (s32[2048]{0:T(1024)}, s32[2048]{0:T(1024)S(1)}) sort(s32[2048]{0:T(1024)S(1)} %add_select_fusion, s32[2048]{0:T(1024)S(1)} %iota.12), dimensions={0}, to_apply=%region_14.15 | sort | flops 22528 | bytes 32768 | tf_op jit(solution)/shard_map/jit(argsort)/sort | solution.py:19
  231.5 20.5 %gather_fusion = s32[2048]{0:T(1024)} fusion(s32[2048]{0:T(1024)S(1)} %copy-done.1, s32[2048]{0:T(1024)S(1)} %get-tuple-element.238), kind=kCustom, calls=%fused_computation | custom fusion | bytes 24576 | tf_op jit(solution)/shard_map/gather | solution.py:20
  252.0 3.3 all-to-all-start
  255.5 6.3 %all-to-all-done = s32[8,1,256]{2,1,0:T(1,128)S(1)} async-done(((s32[8,1,256]{2,1,0:T(1,128)}), s32[8,1,256]{2,1,0:T(1,128)S(1)}, u32[]{:S(2)}, u32[]{:S(2)}) %all-to-all-start) | async-done | bytes 8224 | tf_op jit(solution)/shard_map/all_to_all | solution.py:28
  261.8 10.3 %all-reduce = (f32[2048]{0:T(1024)S(1)}, f32[2048]{0:T(1024)S(1)}) all-reduce(f32[2048]{0:T(1024)S(1)} %get-tuple-element.129, f32[2048]{0:T(1024)S(1)} %get-tuple-element.132), channel_id=1, replica_groups=mesh['cons'=4,'prod'=8] {'cons'}, use_global_device_ids=true, to_apply=%region_13.14 | all-reduce | flops 4096 | bytes 32768 | tf_op jit(solution)/shard_map/psum | solution.py:125
  274.3 5.5 %gather_fusion.2 = f32[2048,64]{1,0:T(8,128)S(1)} fusion(f32[2048,64]{1,0:T(8,128)S(1)} %multiply_subtract_fusion, s32[2048]{0:T(1024)S(1)} %broadcast_clamp_fusion), kind=kCustom, calls=%fused_computation.2 | custom fusion | bytes 1056768 | tf_op jit(solution)/shard_map/jit(_take)/gather | solution.py:29
  280.1 16.6 %all_to_all.20 = f32[8,256,64]{1,2,0:T(8,128)S(1)} all-to-all(f32[8,256,64]{1,2,0:T(8,128)S(1)} %broadcast_select_fusion), channel_id=1, replica_groups=mesh['cons'=4,'prod'=8] {'prod'}, dimensions={0} | all-to-all | bytes 1048576 | tf_op jit(solution)/shard_map/all_to_all | solution.py:31
  297.1 5.8 %scatter_custom_fusion.1 = f32[2048,64]{1,0:T(8,128)S(1)} fusion(s32[2048]{0:T(1024)S(1)} %get-tuple-element.239, f32[2048,64]{1,0:T(8,128)S(1)} %bitcast.110, f32[]{:T(128)} %constant.95.clone.1), kind=kCustom, calls=%fused_computation.49 | custom fusion | bytes 524292 | tf_op jit(solution)/shard_map/scatter | solution.py:35
  302.9 2.0 convolution_bitcast_fusion
  305.9 11.8 %gather_fusion.1 = f32[2048]{0:T(1024)S(1)} fusion(f32[2048]{0:T(1024)S(1)} %broadcast_multiply_fusion.1, s32[2048]{0:T(1024)S(1)} %broadcast_clamp_fusion), kind=kCustom, calls=%fused_computation.1 | custom fusion | bytes 24576 | tf_op jit(solution)/shard_map/jit(_take)/gather | solution.py:30
  317.7 9.9 %all_to_all.21 = f32[8,1,256]{2,1,0:T(1,128)S(1)} all-to-all(f32[8,1,256]{2,1,0:T(1,128)S(1)} %and_select_fusion), channel_id=1, replica_groups=mesh['cons'=4,'prod'=8] {'prod'}, dimensions={0} | all-to-all | bytes 16384 | tf_op jit(solution)/shard_map/all_to_all | solution.py:32
  327.6 8.0 %scatter_custom_fusion = f32[2048]{0:T(1024)S(1)} fusion(s32[2048]{0:T(1024)S(1)} %get-tuple-element.239, f32[2048]{0:T(1024)S(1)} %bitcast.127, f32[]{:T(128)} %constant.95.clone.1), kind=kCustom, calls=%fused_computation.72 | custom fusion | bytes 8196 | tf_op jit(solution)/shard_map/scatter | solution.py:36
  335.7 2.3 fusion.36
  338.0 2.9 copy.29
  (151 shorter events, 29.2 us)
Async XLA Ops:
  7.2 295.8 %copy-start = (f32[16,128,128]{2,1,0:T(8,128)S(1)}, f32[16,128,128]{2,1,0:T(8,128)}, u32[]{:S(2)}) copy-start(f32[16,128,128]{2,1,0:T(8,128)} %param.19) | copy-start | bytes 3145732
  7.2 123.5 %all-reduce.3.cloned.1.call-start = ((), (), s32[]{:S(2)}) async-start(), calls=%async_computation.4 | async-start | bytes 262144 | tf_op jit(solution)/shard_map/psum | solution.py:67
  9.5 262.6 %reduce-scatter.4.cloned.1.call-start = ((), (), s32[]{:S(2)}) async-start(), calls=%async_computation.6 | async-start | bytes 2621440
  64.1 47.6 %copy-start.4 = (f32[4096]{0:T(1024)S(1)}, f32[4096]{0:T(1024)}, u32[]{:S(2)}) copy-start(f32[4096]{0:T(1024)} %param.14) | copy-start | bytes 49156
  64.1 47.6 %copy-start.6 = (s32[256]{0:T(256)S(1)}, s32[256]{0:T(256)}, u32[]{:S(2)}) copy-start(s32[256]{0:T(256)} %param.17) | copy-start | bytes 3076
  133.0 1.9 copy-start.3
  133.0 4.0 %copy-start.5 = (f32[256,128]{1,0:T(8,128)S(1)}, f32[256,128]{1,0:T(8,128)}, u32[]{:S(2)}) copy-start(f32[256,128]{1,0:T(8,128)} %get-tuple-element.472) | copy-start | bytes 393220 | tf_op jit(solution)/shard_map/while
  144.8 1.9 copy-start.3
  144.8 4.0 %copy-start.5 = (f32[256,128]{1,0:T(8,128)S(1)}, f32[256,128]{1,0:T(8,128)}, u32[]{:S(2)}) copy-start(f32[256,128]{1,0:T(8,128)} %get-tuple-element.472) | copy-start | bytes 393220 | tf_op jit(solution)/shard_map/while
  156.5 1.9 copy-start.3
  156.5 4.0 %copy-start.5 = (f32[256,128]{1,0:T(8,128)S(1)}, f32[256,128]{1,0:T(8,128)}, u32[]{:S(2)}) copy-start(f32[256,128]{1,0:T(8,128)} %get-tuple-element.472) | copy-start | bytes 393220 | tf_op jit(solution)/shard_map/while
  168.2 1.9 copy-start.3
  168.2 4.0 %copy-start.5 = (f32[256,128]{1,0:T(8,128)S(1)}, f32[256,128]{1,0:T(8,128)}, u32[]{:S(2)}) copy-start(f32[256,128]{1,0:T(8,128)} %get-tuple-element.472) | copy-start | bytes 393220 | tf_op jit(solution)/shard_map/while
  179.9 1.9 copy-start.3
  180.0 4.0 %copy-start.5 = (f32[256,128]{1,0:T(8,128)S(1)}, f32[256,128]{1,0:T(8,128)}, u32[]{:S(2)}) copy-start(f32[256,128]{1,0:T(8,128)} %get-tuple-element.472) | copy-start | bytes 393220 | tf_op jit(solution)/shard_map/while
  191.7 1.9 copy-start.3
  191.7 4.0 %copy-start.5 = (f32[256,128]{1,0:T(8,128)S(1)}, f32[256,128]{1,0:T(8,128)}, u32[]{:S(2)}) copy-start(f32[256,128]{1,0:T(8,128)} %get-tuple-element.472) | copy-start | bytes 393220 | tf_op jit(solution)/shard_map/while
  203.4 1.9 copy-start.3
  203.4 4.0 %copy-start.5 = (f32[256,128]{1,0:T(8,128)S(1)}, f32[256,128]{1,0:T(8,128)}, u32[]{:S(2)}) copy-start(f32[256,128]{1,0:T(8,128)} %get-tuple-element.472) | copy-start | bytes 393220 | tf_op jit(solution)/shard_map/while
  215.1 1.9 copy-start.3
  215.1 4.0 %copy-start.5 = (f32[256,128]{1,0:T(8,128)S(1)}, f32[256,128]{1,0:T(8,128)}, u32[]{:S(2)}) copy-start(f32[256,128]{1,0:T(8,128)} %get-tuple-element.472) | copy-start | bytes 393220 | tf_op jit(solution)/shard_map/while
  224.5 1.9 copy-start.1
  252.0 9.8 %all-to-all-start = ((s32[8,1,256]{2,1,0:T(1,128)}), s32[8,1,256]{2,1,0:T(1,128)S(1)}, u32[]{:S(2)}, u32[]{:S(2)}) async-start(s32[8,1,256]{2,1,0:T(1,128)} %bitcast.8), calls=%async_computation | async-start | bytes 16384 | tf_op jit(solution)/shard_map/all_to_all | solution.py:28
  255.3 82.7 %all-gather.3.cloned.1.call-start = ((), (), s32[]{:S(2)}) async-start(), calls=%async_computation.5 | async-start | bytes 2621440 | tf_op jit(solution)/shard_map/all_gather | solution.py:132
  305.9 11.8 %copy-start.2 = (f32[2048]{0:T(1024)}, f32[2048]{0:T(1024)S(1)}, u32[]{:S(2)}) copy-start(f32[2048]{0:T(1024)S(1)} %broadcast_multiply_fusion.1) | copy-start | bytes 24580
Sparse Core Ops, SparseCore 0:
  11.9 73.2 all-reduce.2
  226.5 29.7 reduce-scatter.3
  306.0 20.7 all-gather.2
